TPU v7x, 512 devices: a whole 4x4x16 slice. The times are simulated.
512 devices in a mesh: obj: 16 (over x, z_hi, core), tile: 32 (over y, z_lo).
Axes of the slice: x: 4, y: 4, z: 16 (z_hi: 2, z_lo: 8; z = z_hi * 8 + z_lo), core: 2. Of those that a mesh axis runs over, the one named last changes fastest.
Arguments:
- checkpoints: bfloat16 [6, 12, 48, 32, 128], P(None, None, 'obj', 'tile'), may hold values from 0.19921875 to 2
- courant: float32 [2, 48, 32, 128], P(None, None, 'tile'), may hold values from -0.6 to 0.6
- insolation: float32 [32, 128], P('tile'), may hold values from 0.3 to 3
- region_mask: int32 [16, 32, 128], P('obj', 'tile'), may hold values 0 or 1
- measure_step: int32 [16], P('obj'), may hold values from 1 to 6
- snr_weight: float32 [12, 48], replicated, may hold values from 0.3 to 3
- diffusion_number: float32 [12, 47], replicated, may hold values from 0.1 to 2
- coupling: float32 [12, 12], replicated, may hold values from -1.75 to 1.75
- recombination: float32 [12], replicated, may hold values from 0.05 to 0.25
Outputs:
- state_adjoint: float32 [16, 12, 48, 32, 128], P('obj', None, None, 'tile')
- driver_grad: float32 [16, 6, 12, 48], P('obj')
All inputs are finite; a program needn't handle non-finite values. No bound on the sum of `region_mask` on one device may be relied on, other than what follows from the above.
Results may differ from a plain program's by a relative error of at most 0.0003.
Values may be sent and summed in bfloat16 or wider, within the bound.
A program may use at most 64 MiB of HBM per device.

v0:
```python
import jax
import jax.numpy as jnp
from jax import lax
from jax.sharding import PartitionSpec as P

smoothing = 0.2


def padded_2(block, sides, width):
    for axis, dim in sides:
        count = lax.axis_size(axis)
        forward = [(i, i + 1) for i in range(count - 1)]
        forward.append((count - 1, 0))
        backward = [(target, source) for source, target in forward]
        low = lax.ppermute(
            lax.slice_in_dim(block, block.shape[dim] - width, None, axis=dim), axis, forward
        )
        high = lax.ppermute(lax.slice_in_dim(block, 0, width, axis=dim), axis, backward)
        block = jnp.concatenate([low, block, high], axis=dim)
    return block


def advect_back(adjoint, padded, flux, northward):
    lat_pad = jnp.pad(adjoint, ((0, 0), (0, 0), (0, 0), (1, 1)))
    north_flux = jnp.pad(northward[None] * adjoint, ((0, 0), (0, 0), (0, 0), (1, 1)))
    beside_all = padded[:, :, 2:] + padded[:, :, :-2] + lat_pad[..., 2:] + lat_pad[..., :-2]
    carried = flux[:, :, 2:] - flux[:, :, :-2] + north_flux[..., 2:] - north_flux[..., :-2]
    return (1.0 - 4.0 * smoothing) * adjoint + smoothing * beside_all + 0.5 * carried


def react_back(solved, state, coupling, recombination):
    mixing = jnp.einsum("fg,...flxy->...glxy", coupling, solved, precision=lax.Precision.HIGHEST)
    return (
        solved
        + mixing
        - 2.0 * recombination[:, None, None, None] * state.astype(jnp.float32) * solved
    )


def per_device(
    checkpoints,
    courant,
    insolation,
    region_mask,
    measure_step,
    snr_weight,
    diffusion_number,
    coupling,
    recombination,
):
    steps = checkpoints.shape[0]
    fields, levels = snr_weight.shape
    width, latitudes = insolation.shape
    columns = width * latitudes
    cells = columns * lax.axis_size("tile")
    impulse = region_mask[0].astype(jnp.float32)[None, None] * snr_weight[:, :, None, None]
    below = jnp.pad(diffusion_number, ((0, 0), (1, 0)))
    above = jnp.pad(diffusion_number, ((0, 0), (0, 1)))
    middle = 1.0 + below + above
    eastward = courant[0]
    northward = courant[1]
    adjoint = jnp.zeros((fields, levels, width, latitudes), jnp.float32)
    partials = [None] * steps
    for back in range(steps):
        moment = steps - 1 - back
        arrive = (measure_step[0] == moment + 1).astype(jnp.float32)
        adjoint = adjoint + arrive * impulse
        stacked = jnp.stack([adjoint, eastward[None] * adjoint])
        extended = padded_2(stacked, (("tile", 3),), 1)
        padded = extended[0]
        flux = extended[1]
        advected = advect_back(adjoint, padded, flux, northward)
        solved = lax.linalg.tridiagonal_solve(
            -below, middle, -above, advected.reshape(fields, levels, columns)
        )
        solved = solved.reshape(fields, levels, width, latitudes)
        partial_sum = jnp.einsum("flxy,xy->fl", solved, insolation, precision=lax.Precision.HIGHEST)
        partial_sum = lax.psum(partial_sum, "tile")
        partials[moment] = partial_sum
        state = checkpoints[moment]
        adjoint = react_back(
            solved, lax.all_gather(state, "obj", axis=1, tiled=True), coupling, recombination
        )
    gradients = jnp.stack(partials)
    return (adjoint[None], (gradients / cells)[None])


def solution(mesh):
    return jax.shard_map(
        per_device,
        mesh=mesh,
        in_specs=(
            P(None, None, "obj", "tile", None),
            P(None, None, "tile", None),
            P("tile", None),
            P("obj", "tile", None),
            P("obj"),
            P(),
            P(),
            P(),
            P(),
        ),
        out_specs=(P("obj", None, None, "tile", None), P("obj", None, None, None)),
        check_vma=False,
    )
```

profile of v0, /device:TPU:2, one launch (start us, length us, event | category | flops | bytes accessed | tf_op | source)
XLA Modules:
  0.0 679.5 jit_solution(14576754906486607328)
XLA Ops:
  2.0 0.8 copy.28
  2.8 0.8 fusion.1314
  4.0 15.6 %collective-permute-start.1 = (f32[2,12,48,1,128]{4,2,3,1,0:T(8,128)S(1)}, f32[2,12,48,1,128]{4,2,3,1,0:T(8,128)S(1)}, u32[]{:S(2)}, u32[]{:S(2)}) collective-permute-start(f32[2,12,48,1,128]{4,2,3,1,0:T(8,128)S(1)} %copy.30), channel_id=1, source_target_pairs={{1,0},{2,1},{3,2},{4,3},{5,4},{6,5},{7,6},{8,7},{9,8},{10,9},{11,1... | collective-permute-start | bytes 1769480 | tf_op jit(solution)/shard_map/ppermute | solution.py:18
  19.6 1.9 collective-permute-start
  22.8 53.9 %all-gather = bf16[1,12,48,1,128]{4,1,3,0,2:T(8,128)(2,1)S(1)} all-gather(bf16[1,12,3,1,128]{4,1,3,0,2:T(8,128)(2,1)S(1)} %copy.99), channel_id=2, replica_groups=mesh['obj'=16,'tile'=32] {'obj'}, dimensions={2}, use_global_device_ids=true | all-gather | bytes 156672 | tf_op jit(solution)/shard_map/all_gather | solution.py:82
  82.4 3.4 collective-permute-start.3
  85.8 2.5 collective-permute-start.2
  88.3 57.2 %all-gather.1 = bf16[1,12,48,1,128]{4,1,3,0,2:T(8,128)(2,1)S(1)} all-gather(bf16[1,12,3,1,128]{4,1,3,0,2:T(8,128)(2,1)S(1)} %copy.100), channel_id=3, replica_groups=mesh['obj'=16,'tile'=32] {'obj'}, dimensions={2}, use_global_device_ids=true | all-gather | bytes 156672 | tf_op jit(solution)/shard_map/all_gather | solution.py:82
  151.0 4.8 collective-permute-start.5
  155.8 1.9 collective-permute-start.4
  157.7 57.7 %all-gather.2 = bf16[1,12,48,1,128]{4,1,3,0,2:T(8,128)(2,1)S(1)} all-gather(bf16[1,12,3,1,128]{4,1,3,0,2:T(8,128)(2,1)S(1)} %copy.101), channel_id=4, replica_groups=mesh['obj'=16,'tile'=32] {'obj'}, dimensions={2}, use_global_device_ids=true | all-gather | bytes 156672 | tf_op jit(solution)/shard_map/all_gather | solution.py:82
  221.0 5.3 collective-permute-start.7
  226.3 1.9 collective-permute-start.6
  228.3 58.2 %all-gather.5 = bf16[1,12,48,1,128]{4,1,3,0,2:T(8,128)(2,1)S(1)} all-gather(bf16[1,12,3,1,128]{4,1,3,0,2:T(8,128)(2,1)S(1)} %copy.104), channel_id=7, replica_groups=mesh['obj'=16,'tile'=32] {'obj'}, dimensions={2}, use_global_device_ids=true | all-gather | bytes 156672 | tf_op jit(solution)/shard_map/all_gather | solution.py:82
  286.5 34.6 %all-gather.3 = bf16[1,12,48,1,128]{4,1,3,0,2:T(8,128)(2,1)S(1)} all-gather(bf16[1,12,3,1,128]{4,1,3,0,2:T(8,128)(2,1)S(1)} %copy.102), channel_id=5, replica_groups=mesh['obj'=16,'tile'=32] {'obj'}, dimensions={2}, use_global_device_ids=true | all-gather | bytes 156672 | tf_op jit(solution)/shard_map/all_gather | solution.py:82
  321.0 45.1 %all-gather.4 = bf16[1,12,48,1,128]{4,1,3,0,2:T(8,128)(2,1)S(1)} all-gather(bf16[1,12,3,1,128]{4,1,3,0,2:T(8,128)(2,1)S(1)} %copy.103), channel_id=6, replica_groups=mesh['obj'=16,'tile'=32] {'obj'}, dimensions={2}, use_global_device_ids=true | all-gather | bytes 156672 | tf_op jit(solution)/shard_map/all_gather | solution.py:82
  366.1 0.9 fusion.84
  372.7 7.7 %collective-permute-start.9 = (f32[2,12,48,1,128]{4,2,3,1,0:T(8,128)S(1)}, f32[2,12,48,1,128]{4,2,3,1,0:T(8,128)S(1)}, u32[]{:S(2)}, u32[]{:S(2)}) collective-permute-start(f32[2,12,48,1,128]{4,2,3,1,0:T(8,128)S(1)} %copy.60), channel_id=1, source_target_pairs={{1,0},{2,1},{3,2},{4,3},{5,4},{6,5},{7,6},{8,7},{9,8},{10,9},{11,1... | collective-permute-start | bytes 1769480 | tf_op jit(solution)/shard_map/ppermute | solution.py:18
  380.4 2.1 collective-permute-start.8
  382.6 0.9 fusion.86
  383.6 0.9 fusion.88
  384.6 9.5 %collective-permute-done.9 = f32[2,12,48,1,128]{4,2,3,1,0:T(8,128)S(1)} collective-permute-done((f32[2,12,48,1,128]{4,2,3,1,0:T(8,128)S(1)}, f32[2,12,48,1,128]{4,2,3,1,0:T(8,128)S(1)}, u32[]{:S(2)}, u32[]{:S(2)}) %collective-permute-start.9) | collective-permute-done | bytes 589856 | tf_op jit(solution)/shard_map/ppermute | solution.py:18
  394.3 12.6 %collective-permute-done.8 = f32[2,12,48,1,128]{4,2,3,1,0:T(8,128)S(1)} collective-permute-done((f32[2,12,48,1,128]{4,2,3,1,0:T(8,128)S(1)}, f32[2,12,48,1,128]{4,2,3,1,0:T(8,128)S(1)}, u32[]{:S(2)}, u32[]{:S(2)}) %collective-permute-start.8) | collective-permute-done | bytes 589856 | tf_op jit(solution)/shard_map/ppermute | solution.py:15
  412.2 5.6 collective-permute-start.11
  417.8 1.9 collective-permute-start.10
  419.7 0.9 fusion.90
  420.8 0.9 fusion.92
  421.7 19.9 %collective-permute-done.11 = f32[2,12,48,1,128]{4,2,3,1,0:T(8,128)S(1)} collective-permute-done((f32[2,12,48,1,128]{4,2,3,1,0:T(8,128)S(1)}, f32[2,12,48,1,128]{4,2,3,1,0:T(8,128)S(1)}, u32[]{:S(2)}, u32[]{:S(2)}) %collective-permute-start.11) | collective-permute-done | bytes 589856 | tf_op jit(solution)/shard_map/ppermute | solution.py:18
  441.9 1.7 collective-permute-done.10
  448.5 1.0 copy.74
  449.6 0.9 fusion.94
  450.5 228.3 %all-reduce.14 = (f32[1,1,12,48]{3,0,2,1:T(1,128)S(1)}, f32[1,1,12,48]{3,0,2,1:T(1,128)S(1)}, f32[1,1,12,48]{3,0,2,1:T(1,128)S(1)}, f32[1,1,12,48]{3,0,2,1:T(1,1...) all-reduce(f32[1,1,12,48]{3,0,2,1:T(1,128)S(1)} %stack.87, ...), channel_id=1, replica_groups=mesh['obj'=16,'tile'=32] {'tile'}, use_global_device_ids=true, to_apply=%region_0.1 | all-reduce | flops 3456 | bytes 27648 | tf_op jit(solution)/shard_map/psum | solution.py:78
  (414 shorter events, 35.6 us)
Async XLA Ops:
  0.6 80.8 %copy-start = (f32[12,12]{1,0:T(8,128)S(1)}, f32[12,12]{1,0:T(8,128)}, u32[]{:S(2)}) copy-start(f32[12,12]{1,0:T(8,128)} %param.16) | copy-start | bytes 1732
  0.6 20.9 %copy-start.3 = (f32[12,47]{1,0:T(8,128)S(1)}, f32[12,47]{1,0:T(8,128)}, u32[]{:S(2)}) copy-start(f32[12,47]{1,0:T(8,128)} %param.15) | copy-start | bytes 6772
  0.7 21.1 %copy-start.1 = (bf16[6,12,3,1,128]{4,2,3,1,0:T(4,128)(2,1)S(1)}, bf16[6,12,3,1,128]{4,2,3,1,0:T(4,128)(2,1)}, u32[]{:S(2)}) copy-start(bf16[6,12,3,1,128]{4,2,3,1,0:T(4,128)(2,1)} %param.9) | copy-start | bytes 165892
  0.7 22.1 %copy-start.4 = (f32[12]{0:T(128)S(1)}, f32[12]{0:T(128)}, u32[]{:S(2)}) copy-start(f32[12]{0:T(128)} %param.17) | copy-start | bytes 148
  4.0 72.9 %collective-permute-start.1 = (f32[2,12,48,1,128]{4,2,3,1,0:T(8,128)S(1)}, f32[2,12,48,1,128]{4,2,3,1,0:T(8,128)S(1)}, u32[]{:S(2)}, u32[]{:S(2)}) collective-permute-start(f32[2,12,48,1,128]{4,2,3,1,0:T(8,128)S(1)} %copy.30), channel_id=1, source_target_pairs={{1,0},{2,1},{3,2},{4,3},{5,4},{6,5},{7,6},{8,7},{9,8},{10,9},{11,1... | collective-permute-start | bytes 1769480 | tf_op jit(solution)/shard_map/ppermute | solution.py:18
  19.6 57.5 %collective-permute-start = (f32[2,12,48,1,128]{4,2,3,1,0:T(8,128)S(1)}, f32[2,12,48,1,128]{4,2,3,1,0:T(8,128)S(1)}, u32[]{:S(2)}, u32[]{:S(2)}) collective-permute-start(f32[2,12,48,1,128]{4,2,3,1,0:T(8,128)S(1)} %copy.30), channel_id=1, source_target_pairs={{0,1},{1,2},{2,3},{3,4},{4,5},{5,6},{6,7},{7,8},{8,9},{9,10},{10,1... | collective-permute-start | bytes 1769480 | tf_op jit(solution)/shard_map/ppermute | solution.py:15
  82.4 63.0 %collective-permute-start.3 = (f32[2,12,48,1,128]{4,2,3,1,0:T(8,128)S(1)}, f32[2,12,48,1,128]{4,2,3,1,0:T(8,128)S(1)}, u32[]{:S(2)}, u32[]{:S(2)}) collective-permute-start(f32[2,12,48,1,128]{4,2,3,1,0:T(8,128)S(1)} %copy.39), channel_id=1, source_target_pairs={{1,0},{2,1},{3,2},{4,3},{5,4},{6,5},{7,6},{8,7},{9,8},{10,9},{11,1... | collective-permute-start | bytes 1769480 | tf_op jit(solution)/shard_map/ppermute | solution.py:18
  85.8 59.8 %collective-permute-start.2 = (f32[2,12,48,1,128]{4,2,3,1,0:T(8,128)S(1)}, f32[2,12,48,1,128]{4,2,3,1,0:T(8,128)S(1)}, u32[]{:S(2)}, u32[]{:S(2)}) collective-permute-start(f32[2,12,48,1,128]{4,2,3,1,0:T(8,128)S(1)} %copy.39), channel_id=1, source_target_pairs={{0,1},{1,2},{2,3},{3,4},{4,5},{5,6},{6,7},{7,8},{8,9},{9,10},{10,1... | collective-permute-start | bytes 1769480 | tf_op jit(solution)/shard_map/ppermute | solution.py:15
  151.0 64.5 %collective-permute-start.5 = (f32[2,12,48,1,128]{4,2,3,1,0:T(8,128)S(1)}, f32[2,12,48,1,128]{4,2,3,1,0:T(8,128)S(1)}, u32[]{:S(2)}, u32[]{:S(2)}) collective-permute-start(f32[2,12,48,1,128]{4,2,3,1,0:T(8,128)S(1)} %copy.46), channel_id=1, source_target_pairs={{1,0},{2,1},{3,2},{4,3},{5,4},{6,5},{7,6},{8,7},{9,8},{10,9},{11,1... | collective-permute-start | bytes 1769480 | tf_op jit(solution)/shard_map/ppermute | solution.py:18
  155.8 59.9 %collective-permute-start.4 = (f32[2,12,48,1,128]{4,2,3,1,0:T(8,128)S(1)}, f32[2,12,48,1,128]{4,2,3,1,0:T(8,128)S(1)}, u32[]{:S(2)}, u32[]{:S(2)}) collective-permute-start(f32[2,12,48,1,128]{4,2,3,1,0:T(8,128)S(1)} %copy.46), channel_id=1, source_target_pairs={{0,1},{1,2},{2,3},{3,4},{4,5},{5,6},{6,7},{7,8},{8,9},{9,10},{10,1... | collective-permute-start | bytes 1769480 | tf_op jit(solution)/shard_map/ppermute | solution.py:15
  220.8 145.4 %copy-start.2 = (f32[1,128]{1,0:T(1,128)S(1)}, f32[1,128]{1,0:T(1,128)}, u32[]{:S(2)}) copy-start(f32[1,128]{1,0:T(1,128)} %param.11) | copy-start | bytes 1540
  221.0 146.1 %collective-permute-start.7 = (f32[2,12,48,1,128]{4,2,3,1,0:T(8,128)S(1)}, f32[2,12,48,1,128]{4,2,3,1,0:T(8,128)S(1)}, u32[]{:S(2)}, u32[]{:S(2)}) collective-permute-start(f32[2,12,48,1,128]{4,2,3,1,0:T(8,128)S(1)} %copy.53), channel_id=1, source_target_pairs={{1,0},{2,1},{3,2},{4,3},{5,4},{6,5},{7,6},{8,7},{9,8},{10,9},{11,1... | collective-permute-start | bytes 1769480 | tf_op jit(solution)/shard_map/ppermute | solution.py:18
  226.3 141.0 %collective-permute-start.6 = (f32[2,12,48,1,128]{4,2,3,1,0:T(8,128)S(1)}, f32[2,12,48,1,128]{4,2,3,1,0:T(8,128)S(1)}, u32[]{:S(2)}, u32[]{:S(2)}) collective-permute-start(f32[2,12,48,1,128]{4,2,3,1,0:T(8,128)S(1)} %copy.53), channel_id=1, source_target_pairs={{0,1},{1,2},{2,3},{3,4},{4,5},{5,6},{6,7},{7,8},{8,9},{9,10},{10,1... | collective-permute-start | bytes 1769480 | tf_op jit(solution)/shard_map/ppermute | solution.py:15
  372.7 21.4 %collective-permute-start.9 = (f32[2,12,48,1,128]{4,2,3,1,0:T(8,128)S(1)}, f32[2,12,48,1,128]{4,2,3,1,0:T(8,128)S(1)}, u32[]{:S(2)}, u32[]{:S(2)}) collective-permute-start(f32[2,12,48,1,128]{4,2,3,1,0:T(8,128)S(1)} %copy.60), channel_id=1, source_target_pairs={{1,0},{2,1},{3,2},{4,3},{5,4},{6,5},{7,6},{8,7},{9,8},{10,9},{11,1... | collective-permute-start | bytes 1769480 | tf_op jit(solution)/shard_map/ppermute | solution.py:18
  380.4 26.5 %collective-permute-start.8 = (f32[2,12,48,1,128]{4,2,3,1,0:T(8,128)S(1)}, f32[2,12,48,1,128]{4,2,3,1,0:T(8,128)S(1)}, u32[]{:S(2)}, u32[]{:S(2)}) collective-permute-start(f32[2,12,48,1,128]{4,2,3,1,0:T(8,128)S(1)} %copy.60), channel_id=1, source_target_pairs={{0,1},{1,2},{2,3},{3,4},{4,5},{5,6},{6,7},{7,8},{8,9},{9,10},{10,1... | collective-permute-start | bytes 1769480 | tf_op jit(solution)/shard_map/ppermute | solution.py:15
  412.2 29.5 %collective-permute-start.11 = (f32[2,12,48,1,128]{4,2,3,1,0:T(8,128)S(1)}, f32[2,12,48,1,128]{4,2,3,1,0:T(8,128)S(1)}, u32[]{:S(2)}, u32[]{:S(2)}) collective-permute-start(f32[2,12,48,1,128]{4,2,3,1,0:T(8,128)S(1)} %copy.67), channel_id=1, source_target_pairs={{1,0},{2,1},{3,2},{4,3},{5,4},{6,5},{7,6},{8,7},{9,8},{10,9},{11,1... | collective-permute-start | bytes 1769480 | tf_op jit(solution)/shard_map/ppermute | solution.py:18
  417.8 25.8 %collective-permute-start.10 = (f32[2,12,48,1,128]{4,2,3,1,0:T(8,128)S(1)}, f32[2,12,48,1,128]{4,2,3,1,0:T(8,128)S(1)}, u32[]{:S(2)}, u32[]{:S(2)}) collective-permute-start(f32[2,12,48,1,128]{4,2,3,1,0:T(8,128)S(1)} %copy.67), channel_id=1, source_target_pairs={{0,1},{1,2},{2,3},{3,4},{4,5},{5,6},{6,7},{7,8},{8,9},{9,10},{10,1... | collective-permute-start | bytes 1769480 | tf_op jit(solution)/shard_map/ppermute | solution.py:15
where the time goes:
time: 680 us
  blocking collectives  535 us (79%)
  starting transfers between devices  54.6 us (8%)
  waiting for transfers between devices  43.7 us (6%)
  other arithmetic  26.3 us (4%)
  matrix products  9.1 us (1%)
  local copies, waits for them, and re-layouts  8.41 us (1%)
    all_gather x6, blocking collectives, per_device(): lax.all_gather(state, 'obj', axis=1, tiled=True)  307 us
    psum x1, blocking collectives, per_device(): partial_sum = lax.psum(partial_sum, 'tile')  228 us
    ppermute x6, starting transfers between devices, padded_2(): lax.ppermute(lax.slice_in_dim(block, 0, width, axis=dim), axis, backward)  42.3 us
    ppermute x6, waiting for transfers between devices, padded_2(): lax.ppermute(lax.slice_in_dim(block, 0, width, axis=dim), axis, backward)  29.4 us
    unnamed x144, other arithmetic  14.8 us
    ppermute x6, waiting for transfers between devices, padded_2(): lax.ppermute(lax.slice_in_dim(block, block.shape[dim] - width, None, axis...  14.3 us
  transfers between devices with their start and end apart: 12, of which 4 were waited for; matrix products, arithmetic and copies ran while one was open for 1% of the time, Pallas kernels for 0%

commit v1 on v0

--- a/solution.py
+++ b/solution.py
@@ -75,7 +75,8 @@
         )
         solved = solved.reshape(fields, levels, width, latitudes)
         partial_sum = jnp.einsum("flxy,xy->fl", solved, insolation, precision=lax.Precision.HIGHEST)
-        partial_sum = lax.psum(partial_sum, "tile")
+        local_part = lax.all_gather(partial_sum, "tile")
+        partial_sum = jnp.sum(local_part, 0)
         partials[moment] = partial_sum
         state = checkpoints[moment]
         adjoint = react_back(

time: 680 us -> 1320 us (1.94)
  blocking collectives: 535 us -> 1010 us
  other arithmetic: 26.3 us -> 181 us
  waiting for transfers between devices: 43.7 us -> 0.03 us
  local copies, waits for them, and re-layouts: 8.41 us -> 50.1 us
    all_gather x0 -> x6, blocking collectives: none -> 705 us  [per_device(): local_part = lax.all_gather(partial_sum, 'tile')]
    psum x1 -> x0, blocking collectives: 228 us -> none  [per_device(): partial_sum = lax.psum(partial_sum, 'tile')]
    unnamed x144, other arithmetic: 14.8 us -> 146 us
    unnamed x156 -> x468, local copies, waits for them, and re-layouts: 2.21 us -> 42.1 us
    ppermute x6, waiting for transfers between devices: 29.4 us -> 0.02 us  [padded_2(): lax.ppermute(lax.slice_in_dim(block, 0, width, axis=dim), axis, backward)]
    ppermute x6, waiting for transfers between devices: 14.3 us -> 0.02 us  [padded_2(): lax.ppermute(lax.slice_in_dim(block, block.shape[dim] - width, None, axis...]
  transfers between devices with their start and end apart: 12 -> 12, of which waited for: 4 -> 0; matrix products, arithmetic and copies ran while one was open for 1% -> 2% of each run, Pallas kernels for 0% -> 0%
where the time goes in v1:
time: 1320 us; the launch traced here: 1310 us
  blocking collectives  1010 us (77%)
  other arithmetic  181 us (14%)
  local copies, waits for them, and re-layouts  50.1 us (4%)
  starting transfers between devices  47.5 us (4%)
  matrix products  15.9 us (1%)
    all_gather x6, blocking collectives, per_device(): local_part = lax.all_gather(partial_sum, 'tile')  705 us
    all_gather x6, blocking collectives, per_device(): lax.all_gather(state, 'obj', axis=1, tiled=True)  304 us
    unnamed x144, other arithmetic  146 us
    unnamed x468, local copies, waits for them, and re-layouts  42.1 us
    ppermute x6, starting transfers between devices, padded_2(): lax.ppermute(lax.slice_in_dim(block, 0, width, axis=dim), axis, backward)  35.1 us
  transfers between devices with their start and end apart: 12, of which 0 were waited for; matrix products, arithmetic and copies ran while one was open for 2% of the time, Pallas kernels for 0%

profile of v1, /device:TPU:2, one launch (start us, length us, event | category | flops | bytes accessed | tf_op | source)
XLA Modules:
  0.0 1308.0 jit_solution(6375031107303281486)
XLA Ops:
  5.2 15.6 %collective-permute-start.1 = (f32[2,12,48,1,128]{4,2,3,1,0:T(8,128)S(1)}, f32[2,12,48,1,128]{4,2,3,1,0:T(8,128)S(1)}, u32[]{:S(2)}, u32[]{:S(2)}) collective-permute-start(f32[2,12,48,1,128]{4,2,3,1,0:T(8,128)S(1)} %copy.30), channel_id=1, source_target_pairs={{1,0},{2,1},{3,2},{4,3},{5,4},{6,5},{7,6},{8,7},{9,8},{10,9},{11,1... | collective-permute-start | bytes 1769480 | tf_op jit(solution)/shard_map/ppermute | solution.py:18
  20.8 1.9 collective-permute-start
  29.2 48.8 %all-gather = bf16[1,12,48,1,128]{4,1,3,0,2:T(8,128)(2,1)S(1)} all-gather(bf16[1,12,3,1,128]{4,1,3,0,2:T(8,128)(2,1)S(1)} %copy.99), channel_id=2, replica_groups=mesh['obj'=16,'tile'=32] {'obj'}, dimensions={2}, use_global_device_ids=true | all-gather | bytes 156672 | tf_op jit(solution)/shard_map/all_gather | solution.py:83
  80.2 2.0 fusion.1138
  101.1 4.3 collective-permute-start.3
  105.5 1.9 collective-permute-start.2
  107.4 57.5 %all-gather.1 = bf16[1,12,48,1,128]{4,1,3,0,2:T(8,128)(2,1)S(1)} all-gather(bf16[1,12,3,1,128]{4,1,3,0,2:T(8,128)(2,1)S(1)} %copy.100), channel_id=3, replica_groups=mesh['obj'=16,'tile'=32] {'obj'}, dimensions={2}, use_global_device_ids=true | all-gather | bytes 156672 | tf_op jit(solution)/shard_map/all_gather | solution.py:83
  166.4 2.6 fusion.959
  188.1 4.0 collective-permute-start.5
  194.1 57.7 %all-gather.5 = bf16[1,12,48,1,128]{4,1,3,0,2:T(8,128)(2,1)S(1)} all-gather(bf16[1,12,3,1,128]{4,1,3,0,2:T(8,128)(2,1)S(1)} %copy.104), channel_id=7, replica_groups=mesh['obj'=16,'tile'=32] {'obj'}, dimensions={2}, use_global_device_ids=true | all-gather | bytes 156672 | tf_op jit(solution)/shard_map/all_gather | solution.py:83
  251.8 36.6 %all-gather.2 = bf16[1,12,48,1,128]{4,1,3,0,2:T(8,128)(2,1)S(1)} all-gather(bf16[1,12,3,1,128]{4,1,3,0,2:T(8,128)(2,1)S(1)} %copy.101), channel_id=4, replica_groups=mesh['obj'=16,'tile'=32] {'obj'}, dimensions={2}, use_global_device_ids=true | all-gather | bytes 156672 | tf_op jit(solution)/shard_map/all_gather | solution.py:83
  289.9 2.0 fusion.786
  291.9 2.2 constant_dynamic-update-slice_fusion.140
  333.1 1.9 constant_dynamic-update-slice_fusion.98
  339.7 4.2 collective-permute-start.7
  345.8 58.3 %all-gather.3 = bf16[1,12,48,1,128]{4,1,3,0,2:T(8,128)(2,1)} all-gather(bf16[1,12,3,1,128]{4,1,3,0,2:T(8,128)(2,1)S(1)} %copy.102), channel_id=5, replica_groups=mesh['obj'=16,'tile'=32] {'obj'}, dimensions={2}, use_global_device_ids=true | all-gather | bytes 156672 | tf_op jit(solution)/shard_map/all_gather | solution.py:83
  404.0 45.6 %all-gather.4 = bf16[1,12,48,1,128]{4,1,3,0,2:T(8,128)(2,1)} all-gather(bf16[1,12,3,1,128]{4,1,3,0,2:T(8,128)(2,1)S(1)} %copy.103), channel_id=6, replica_groups=mesh['obj'=16,'tile'=32] {'obj'}, dimensions={2}, use_global_device_ids=true | all-gather | bytes 156672 | tf_op jit(solution)/shard_map/all_gather | solution.py:83
  450.6 114.7 %all-gather.17 = f32[32,12,48]{2,1,0:T(8,128)S(1)} all-gather(f32[1,12,48]{2,1,0:T(8,128)S(1)} %copy.92), channel_id=13, replica_groups=mesh['obj'=16,'tile'=32] {'tile'}, dimensions={0}, use_global_device_ids=true | all-gather | bytes 76032 | tf_op jit(solution)/shard_map/all_gather | solution.py:78
  569.2 2.0 fusion.613
  571.2 2.2 constant_dynamic-update-slice_fusion.187
  618.4 3.2 collective-permute-start.9
  621.7 2.6 collective-permute-start.8
  625.3 123.5 %all-gather.16 = f32[32,12,48]{2,1,0:T(8,128)S(1)} all-gather(f32[1,12,48]{2,1,0:T(8,128)S(1)} %copy.90), channel_id=12, replica_groups=mesh['obj'=16,'tile'=32] {'tile'}, dimensions={0}, use_global_device_ids=true | all-gather | bytes 76032 | tf_op jit(solution)/shard_map/all_gather | solution.py:78
  752.0 113.7 %all-gather.15 = f32[32,12,48]{2,1,0:T(8,128)S(1)} all-gather(f32[1,12,48]{2,1,0:T(8,128)S(1)} %copy.88), channel_id=11, replica_groups=mesh['obj'=16,'tile'=32] {'tile'}, dimensions={0}, use_global_device_ids=true | all-gather | bytes 76032 | tf_op jit(solution)/shard_map/all_gather | solution.py:78
  869.6 2.0 fusion.440
  871.6 2.2 constant_dynamic-update-slice_fusion.234
  918.8 3.7 collective-permute-start.11
  922.6 2.1 collective-permute-start.10
  925.7 124.0 %all-gather.14 = f32[32,12,48]{2,1,0:T(8,128)S(1)} all-gather(f32[1,12,48]{2,1,0:T(8,128)S(1)} %copy.86), channel_id=10, replica_groups=mesh['obj'=16,'tile'=32] {'tile'}, dimensions={0}, use_global_device_ids=true | all-gather | bytes 76032 | tf_op jit(solution)/shard_map/all_gather | solution.py:78
  1052.9 113.6 %all-gather.13 = f32[32,12,48]{2,1,0:T(8,128)S(1)} all-gather(f32[1,12,48]{2,1,0:T(8,128)S(1)} %copy.84), channel_id=9, replica_groups=mesh['obj'=16,'tile'=32] {'tile'}, dimensions={0}, use_global_device_ids=true | all-gather | bytes 76032 | tf_op jit(solution)/shard_map/all_gather | solution.py:78
  1169.1 2.0 fusion.267
  1191.7 115.2 %all-gather.12 = f32[32,12,48]{2,1,0:T(8,128)S(1)} all-gather(f32[1,12,48]{2,1,0:T(8,128)S(1)} %copy.82), channel_id=8, replica_groups=mesh['obj'=16,'tile'=32] {'tile'}, dimensions={0}, use_global_device_ids=true | all-gather | bytes 76032 | tf_op jit(solution)/shard_map/all_gather | solution.py:78
  (731 shorter events, 229.3 us)
Async XLA Ops:
  3.4 334.3 %copy-start.2 = (f32[12,48]{0,1:T(8,128)}, f32[12,48]{0,1:T(8,128)S(1)}, u32[]{:S(2)}) copy-start(f32[12,48]{0,1:T(8,128)S(1)} %copy.28) | copy-start | bytes 6916
  5.2 73.6 %collective-permute-start.1 = (f32[2,12,48,1,128]{4,2,3,1,0:T(8,128)S(1)}, f32[2,12,48,1,128]{4,2,3,1,0:T(8,128)S(1)}, u32[]{:S(2)}, u32[]{:S(2)}) collective-permute-start(f32[2,12,48,1,128]{4,2,3,1,0:T(8,128)S(1)} %copy.30), channel_id=1, source_target_pairs={{1,0},{2,1},{3,2},{4,3},{5,4},{6,5},{7,6},{8,7},{9,8},{10,9},{11,1... | collective-permute-start | bytes 1769480 | tf_op jit(solution)/shard_map/ppermute | solution.py:18
  20.8 58.2 %collective-permute-start = (f32[2,12,48,1,128]{4,2,3,1,0:T(8,128)S(1)}, f32[2,12,48,1,128]{4,2,3,1,0:T(8,128)S(1)}, u32[]{:S(2)}, u32[]{:S(2)}) collective-permute-start(f32[2,12,48,1,128]{4,2,3,1,0:T(8,128)S(1)} %copy.30), channel_id=1, source_target_pairs={{0,1},{1,2},{2,3},{3,4},{4,5},{5,6},{6,7},{7,8},{8,9},{9,10},{10,1... | collective-permute-start | bytes 1769480 | tf_op jit(solution)/shard_map/ppermute | solution.py:15
  23.5 309.2 %copy-start.22 = (f32[12]{0:T(128)}, f32[12]{0:T(128)S(1)}, u32[]{:S(2)}) copy-start(f32[12]{0:T(128)S(1)} %get-tuple-element.716) | copy-start | bytes 148
  23.5 309.2 %copy-start.25 = (f32[12]{0:T(128)}, f32[12]{0:T(128)S(1)}, u32[]{:S(2)}) copy-start(f32[12]{0:T(128)S(1)} %get-tuple-element.717) | copy-start | bytes 148
  23.5 309.2 %copy-start.28 = (f32[12]{0:T(128)}, f32[12]{0:T(128)S(1)}, u32[]{:S(2)}) copy-start(f32[12]{0:T(128)S(1)} %get-tuple-element.719) | copy-start | bytes 148
  23.6 309.2 %copy-start.31 = (f32[12]{0:T(128)}, f32[12]{0:T(128)S(1)}, u32[]{:S(2)}) copy-start(f32[12]{0:T(128)S(1)} %get-tuple-element.721) | copy-start | bytes 148
  23.6 309.2 %copy-start.34 = (f32[12]{0:T(128)}, f32[12]{0:T(128)S(1)}, u32[]{:S(2)}) copy-start(f32[12]{0:T(128)S(1)} %get-tuple-element.723) | copy-start | bytes 148
  24.9 307.9 %copy-start.37 = (f32[12]{0:T(128)}, f32[12]{0:T(128)S(1)}, u32[]{:S(2)}) copy-start(f32[12]{0:T(128)S(1)} %get-tuple-element.697) | copy-start | bytes 148
  24.9 307.9 %copy-start.41 = (f32[12]{0:T(128)}, f32[12]{0:T(128)S(1)}, u32[]{:S(2)}) copy-start(f32[12]{0:T(128)S(1)} %get-tuple-element.712) | copy-start | bytes 148
  24.9 307.9 %copy-start.45 = (f32[12]{0:T(128)}, f32[12]{0:T(128)S(1)}, u32[]{:S(2)}) copy-start(f32[12]{0:T(128)S(1)} %get-tuple-element.714) | copy-start | bytes 148
  26.2 306.5 %copy-start.49 = (f32[12]{0:T(128)}, f32[12]{0:T(128)S(1)}, u32[]{:S(2)}) copy-start(f32[12]{0:T(128)S(1)} %get-tuple-element.633) | copy-start | bytes 148
  28.3 304.5 %copy-start.7 = (f32[12,1]{0,1:T(1,128)}, f32[12,1]{0,1:T(1,128)S(1)}, u32[]{:S(2)}) copy-start(f32[12,1]{0,1:T(1,128)S(1)} %get-tuple-element.617) | copy-start | bytes 148
  28.3 304.5 %copy-start.10 = (f32[12,1]{0,1:T(1,128)}, f32[12,1]{0,1:T(1,128)S(1)}, u32[]{:S(2)}) copy-start(f32[12,1]{0,1:T(1,128)S(1)} %get-tuple-element.621) | copy-start | bytes 148
  28.4 304.5 %copy-start.13 = (f32[12,1]{0,1:T(1,128)}, f32[12,1]{0,1:T(1,128)S(1)}, u32[]{:S(2)}) copy-start(f32[12,1]{0,1:T(1,128)S(1)} %get-tuple-element.625) | copy-start | bytes 148
  28.4 304.5 %copy-start.16 = (f32[12,1]{0,1:T(1,128)}, f32[12,1]{0,1:T(1,128)S(1)}, u32[]{:S(2)}) copy-start(f32[12,1]{0,1:T(1,128)S(1)} %get-tuple-element.629) | copy-start | bytes 148
  28.4 304.5 %copy-start.19 = (f32[12,1]{0,1:T(1,128)}, f32[12,1]{0,1:T(1,128)S(1)}, u32[]{:S(2)}) copy-start(f32[12,1]{0,1:T(1,128)S(1)} %get-tuple-element.632) | copy-start | bytes 148
  28.4 304.5 %copy-start.53 = (f32[12]{0:T(128)}, f32[12]{0:T(128)S(1)}, u32[]{:S(2)}) copy-start(f32[12]{0:T(128)S(1)} %get-tuple-element.550) | copy-start | bytes 148
  28.4 304.5 %copy-start.57 = (f32[12,1]{0,1:T(1,128)}, f32[12,1]{0,1:T(1,128)S(1)}, u32[]{:S(2)}) copy-start(f32[12,1]{0,1:T(1,128)S(1)} %get-tuple-element.552) | copy-start | bytes 148
  28.4 304.5 %copy-start.61 = (f32[12,1]{0,1:T(1,128)}, f32[12,1]{0,1:T(1,128)S(1)}, u32[]{:S(2)}) copy-start(f32[12,1]{0,1:T(1,128)S(1)} %get-tuple-element.554) | copy-start | bytes 148
  28.4 304.5 %copy-start.65 = (f32[12,1]{0,1:T(1,128)}, f32[12,1]{0,1:T(1,128)S(1)}, u32[]{:S(2)}) copy-start(f32[12,1]{0,1:T(1,128)S(1)} %get-tuple-element.556) | copy-start | bytes 148
  28.4 304.5 %copy-start.69 = (f32[12,1]{0,1:T(1,128)}, f32[12,1]{0,1:T(1,128)S(1)}, u32[]{:S(2)}) copy-start(f32[12,1]{0,1:T(1,128)S(1)} %get-tuple-element.558) | copy-start | bytes 148
  101.1 63.8 %collective-permute-start.3 = (f32[2,12,48,1,128]{4,2,3,1,0:T(8,128)S(1)}, f32[2,12,48,1,128]{4,2,3,1,0:T(8,128)S(1)}, u32[]{:S(2)}, u32[]{:S(2)}) collective-permute-start(f32[2,12,48,1,128]{4,2,3,1,0:T(8,128)S(1)} %copy.39), channel_id=1, source_target_pairs={{1,0},{2,1},{3,2},{4,3},{5,4},{6,5},{7,6},{8,7},{9,8},{10,9},{11,1... | collective-permute-start | bytes 1769480 | tf_op jit(solution)/shard_map/ppermute | solution.py:18
  105.5 59.7 %collective-permute-start.2 = (f32[2,12,48,1,128]{4,2,3,1,0:T(8,128)S(1)}, f32[2,12,48,1,128]{4,2,3,1,0:T(8,128)S(1)}, u32[]{:S(2)}, u32[]{:S(2)}) collective-permute-start(f32[2,12,48,1,128]{4,2,3,1,0:T(8,128)S(1)} %copy.39), channel_id=1, source_target_pairs={{0,1},{1,2},{2,3},{3,4},{4,5},{5,6},{6,7},{7,8},{8,9},{9,10},{10,1... | collective-permute-start | bytes 1769480 | tf_op jit(solution)/shard_map/ppermute | solution.py:15
  188.1 100.3 %collective-permute-start.5 = (f32[2,12,48,1,128]{4,2,3,1,0:T(8,128)S(1)}, f32[2,12,48,1,128]{4,2,3,1,0:T(8,128)S(1)}, u32[]{:S(2)}, u32[]{:S(2)}) collective-permute-start(f32[2,12,48,1,128]{4,2,3,1,0:T(8,128)S(1)} %copy.46), channel_id=1, source_target_pairs={{1,0},{2,1},{3,2},{4,3},{5,4},{6,5},{7,6},{8,7},{9,8},{10,9},{11,1... | collective-permute-start | bytes 1769480 | tf_op jit(solution)/shard_map/ppermute | solution.py:18
  192.1 96.5 %collective-permute-start.4 = (f32[2,12,48,1,128]{4,2,3,1,0:T(8,128)S(1)}, f32[2,12,48,1,128]{4,2,3,1,0:T(8,128)S(1)}, u32[]{:S(2)}, u32[]{:S(2)}) collective-permute-start(f32[2,12,48,1,128]{4,2,3,1,0:T(8,128)S(1)} %copy.46), channel_id=1, source_target_pairs={{0,1},{1,2},{2,3},{3,4},{4,5},{5,6},{6,7},{7,8},{8,9},{9,10},{10,1... | collective-permute-start | bytes 1769480 | tf_op jit(solution)/shard_map/ppermute | solution.py:15
  339.7 227.3 %collective-permute-start.7 = (f32[2,12,48,1,128]{4,2,3,1,0:T(8,128)S(1)}, f32[2,12,48,1,128]{4,2,3,1,0:T(8,128)S(1)}, u32[]{:S(2)}, u32[]{:S(2)}) collective-permute-start(f32[2,12,48,1,128]{4,2,3,1,0:T(8,128)S(1)} %copy.53), channel_id=1, source_target_pairs={{1,0},{2,1},{3,2},{4,3},{5,4},{6,5},{7,6},{8,7},{9,8},{10,9},{11,1... | collective-permute-start | bytes 1769480 | tf_op jit(solution)/shard_map/ppermute | solution.py:18
  343.9 223.3 %collective-permute-start.6 = (f32[2,12,48,1,128]{4,2,3,1,0:T(8,128)S(1)}, f32[2,12,48,1,128]{4,2,3,1,0:T(8,128)S(1)}, u32[]{:S(2)}, u32[]{:S(2)}) collective-permute-start(f32[2,12,48,1,128]{4,2,3,1,0:T(8,128)S(1)} %copy.53), channel_id=1, source_target_pairs={{0,1},{1,2},{2,3},{3,4},{4,5},{5,6},{6,7},{7,8},{8,9},{9,10},{10,1... | collective-permute-start | bytes 1769480 | tf_op jit(solution)/shard_map/ppermute | solution.py:15
  618.4 248.9 %collective-permute-start.9 = (f32[2,12,48,1,128]{4,2,3,1,0:T(8,128)S(1)}, f32[2,12,48,1,128]{4,2,3,1,0:T(8,128)S(1)}, u32[]{:S(2)}, u32[]{:S(2)}) collective-permute-start(f32[2,12,48,1,128]{4,2,3,1,0:T(8,128)S(1)} %copy.60), channel_id=1, source_target_pairs={{1,0},{2,1},{3,2},{4,3},{5,4},{6,5},{7,6},{8,7},{9,8},{10,9},{11,1... | collective-permute-start | bytes 1769480 | tf_op jit(solution)/shard_map/ppermute | solution.py:18
  621.7 245.9 %collective-permute-start.8 = (f32[2,12,48,1,128]{4,2,3,1,0:T(8,128)S(1)}, f32[2,12,48,1,128]{4,2,3,1,0:T(8,128)S(1)}, u32[]{:S(2)}, u32[]{:S(2)}) collective-permute-start(f32[2,12,48,1,128]{4,2,3,1,0:T(8,128)S(1)} %copy.60), channel_id=1, source_target_pairs={{0,1},{1,2},{2,3},{3,4},{4,5},{5,6},{6,7},{7,8},{8,9},{9,10},{10,1... | collective-permute-start | bytes 1769480 | tf_op jit(solution)/shard_map/ppermute | solution.py:15
  918.8 248.3 %collective-permute-start.11 = (f32[2,12,48,1,128]{4,2,3,1,0:T(8,128)S(1)}, f32[2,12,48,1,128]{4,2,3,1,0:T(8,128)S(1)}, u32[]{:S(2)}, u32[]{:S(2)}) collective-permute-start(f32[2,12,48,1,128]{4,2,3,1,0:T(8,128)S(1)} %copy.67), channel_id=1, source_target_pairs={{1,0},{2,1},{3,2},{4,3},{5,4},{6,5},{7,6},{8,7},{9,8},{10,9},{11,1... | collective-permute-start | bytes 1769480 | tf_op jit(solution)/shard_map/ppermute | solution.py:18
  922.6 244.8 %collective-permute-start.10 = (f32[2,12,48,1,128]{4,2,3,1,0:T(8,128)S(1)}, f32[2,12,48,1,128]{4,2,3,1,0:T(8,128)S(1)}, u32[]{:S(2)}, u32[]{:S(2)}) collective-permute-start(f32[2,12,48,1,128]{4,2,3,1,0:T(8,128)S(1)} %copy.67), channel_id=1, source_target_pairs={{0,1},{1,2},{2,3},{3,4},{4,5},{5,6},{6,7},{7,8},{8,9},{9,10},{10,1... | collective-permute-start | bytes 1769480 | tf_op jit(solution)/shard_map/ppermute | solution.py:15
  (141 other events, 6971.6 us)
